TPU v7x, 256 devices: a whole 4x4x8 slice. The times are simulated.
256 devices in a mesh: head: 32 (over y, z), dp: 8 (over x, core).
Axes of the slice: x: 4, y: 4, z: 8, core: 2. Of those that a mesh axis runs over, the one named last changes fastest.
Arguments:
- attn_out: bfloat16 [2048, 8192], P('dp', 'head'), may hold values from -6 to 6
- head_mask: int32 [64], P('head'), may hold values from 0 to 1, as said below
- gate_scale: float32 [64], P('head'), may hold values from 0.25 to 2
- w_out: bfloat16 [8192, 8192], P('head', 'dp'), may hold values from -0.09375 to 0.09375
- grad_out: bfloat16 [2048, 8192], P(('dp', 'head')), may hold values from -6 to 6
Outputs:
- proj_out: bfloat16 [2048, 8192], P(('dp', 'head'))
- grad_attn: bfloat16 [2048, 8192], P('dp', 'head')
- grad_w: float32 [8192, 8192], P('head', 'dp')
Inputs may be any that keep to these rules, and one draw needn't show every extreme that they name: `head_mask`: exactly 32 heads are live.
All inputs are finite; a program needn't handle non-finite values.
Results may differ from a plain program's by a relative error of at most 0.0051.
Values may be sent and summed in bfloat16 or wider, within the bound.
No kernel may reach another device: no remote copies, remote signals or barrier semaphores. Data moves between devices by JAX's collectives and lax.ppermute only.
A program may use at most 128 MiB of HBM per device.

v0:
```python
import jax
import jax.numpy as jnp
from jax import lax
from jax.sharding import Mesh, PartitionSpec as P

BF = jnp.bfloat16
F32 = jnp.float32
XC = ("x", "c")


def exchange(v, axes):
    return lax.all_to_all(v, axes, split_axis=0, concat_axis=0, tiled=False)


def shift(v, axis, s):
    n = lax.axis_size(axis)
    return lax.ppermute(v, axis, [(i, (i + s) % n) for i in range(n)])


def relative(v):
    nx = v.shape[0]
    ring = jnp.concatenate([v[::-1], v[::-1]])
    v = lax.dynamic_slice_in_dim(ring, nx - 1 - lax.axis_index("x"), nx, 0)
    return jnp.where(lax.axis_index("c") == 0, v, v[:, ::-1])


def shards(attn_out, head_mask, gate_scale, w_out, grad_out):
    nx, ny, nz, nc = (lax.axis_size(a) for a in "xyzc")
    me = lax.axis_index("y")
    t, r = attn_out.shape
    j, d = grad_out.shape
    n = d // (nx * nc)
    ty = t // ny
    half = r // 2
    g = exchange(grad_out.reshape(j, nx * nc, n).transpose(1, 0, 2), XC)
    g = relative(g.reshape(nx, nc, j, n)).transpose(1, 0, 2, 3)
    gate_vals = head_mask.astype(F32) * gate_scale
    col_gate = jnp.repeat(gate_vals, r // gate_vals.shape[0])
    gated = (attn_out.astype(F32) * col_gate[None, :]).astype(BF).reshape(ny, ty, r)
    a = [lax.dynamic_index_in_dim(gated, (me + s) % ny, 0, keepdims=False) for s in range(ny)]
    a = [a[0]] + [shift(a[s], "y", s) for s in range(1, ny)]
    a = jnp.concatenate(a, axis=1)
    a, g = lax.optimization_barrier((a, g.reshape(nc * nx * j, n)))
    g = lax.all_gather(g, "z", axis=0, tiled=True)
    a = jnp.stack([a] + [shift(a, "x", s) for s in range(1, nx)])
    a = jnp.stack([a, shift(a, "c", 1)])
    w1, w3 = (shift(w_out, "y", 1), shift(w_out, "y", -1))
    w2 = [shift(w1[:half], "y", 1), shift(w3[half:], "y", -1)]
    a, w = lax.optimization_barrier((a, [w_out, w1, *w2, w3]))
    w = jnp.concatenate(w, axis=0)
    a = a.reshape(nc * nx, nz, j, ny * r).transpose(1, 0, 2, 3).reshape(nx * nc * ty, ny * r)
    part = jnp.dot(a, w, preferred_element_type=F32).astype(BF)
    proj = exchange(part.reshape(nz, nc, nx, j, n), "z").astype(F32).sum(axis=0).astype(BF)
    proj = relative(proj.transpose(1, 0, 2, 3)).reshape(nx * nc, j, n)
    proj = exchange(proj, XC)
    proj_out = proj.transpose(1, 0, 2).reshape(j, d)
    back = lax.dot_general(g, w, (((1,), (1,)), ((), ())), preferred_element_type=F32)
    back = back.reshape(nz, nc, nx, j, ny * r).transpose(1, 2, 0, 3, 4)
    own = back[0] + shift(back[1].astype(BF), "c", 1).astype(F32)
    mine = own[0]
    for s in range(1, nx):
        mine = mine + shift(own[s].astype(BF), "x", -s).astype(F32)
    mine = mine.reshape(ty, ny * r)
    mine = [mine[:, s * r : (s + 1) * r] for s in range(ny)]
    mine = [mine[0]] + [shift(mine[s], "y", -s) for s in range(1, ny)]
    ring = jnp.stack(mine + mine[:-1])
    mine = lax.dynamic_slice_in_dim(ring, (ny - me) % ny, ny, 0).reshape(t, r)
    grad_attn = (mine * col_gate[None, :]).astype(BF)
    back, g = lax.optimization_barrier((back, g))
    gw = lax.dot_general(a, g, (((0,), (0,)), ((), ())), preferred_element_type=F32)
    gw = gw.reshape(ny, 2, half, n)
    near = gw[1].at[0].add(shift(gw[2, 0].astype(BF), "y", -1).astype(F32))
    far = gw[3].at[1].add(shift(gw[2, 1].astype(BF), "y", 1).astype(F32))
    near, far = (shift(near.astype(BF), "y", -1), shift(far.astype(BF), "y", 1))
    grad_w = (gw[0] + near.astype(F32) + far.astype(F32)).reshape(r, n)
    return (proj_out, grad_attn, grad_w)


def solution(mesh):
    fine = Mesh(mesh.devices.reshape(4, 8, 4, 2), ("y", "z", "x", "c"))
    dp, head = (XC, ("y", "z"))
    return jax.shard_map(
        shards,
        mesh=fine,
        in_specs=(P(dp, head), P(head), P(head), P(head, dp), P(dp + head, None)),
        out_specs=(P(dp + head, None), P(dp, head), P(head, dp)),
        check_vma=False,
    )
```

profile of v0, /device:TPU:4, one launch (start us, length us, event | category | flops | bytes accessed | tf_op | source)
XLA Modules:
  0.0 123.9 jit_solution(1273256435222813369)
XLA Ops:
  9.0 3.1 %collective-permute-start.2 = (bf16[64,256]{1,0:T(8,128)(2,1)S(1)}, bf16[64,256]{1,0:T(8,128)(2,1)S(1)}, u32[]{:S(2)}, u32[]{:S(2)}) collective-permute-start(bf16[64,256]{1,0:T(8,128)(2,1)S(1)} %get-tuple-element.62), channel_id=1, source_target_pairs={{0,192},{64,0},{128,64},{192,128},{1,193},{65,1},{129,65},{193,129... | collective-permute-start | bytes 98312 | tf_op jit(solution)/shard_map/ppermute | solution.py:17
  13.7 4.8 %all-to-all-start = ((bf16[8,8,1024]{2,1,0:T(8,128)(2,1)}), bf16[8,8,1024]{2,1,0:T(8,128)(2,1)S(1)}, u32[]{:S(2)}, u32[]{:S(2)}) async-start(bf16[8,8,1024]{2,1,0:T(8,128)(2,1)} %bitcast.130), calls=%async_computation | async-start | bytes 262144 | tf_op jit(solution)/shard_map/all_to_all | solution.py:12
  18.5 3.4 %all-to-all-done = bf16[8,8,1024]{2,1,0:T(8,128)(2,1)S(1)} async-done(((bf16[8,8,1024]{2,1,0:T(8,128)(2,1)}), bf16[8,8,1024]{2,1,0:T(8,128)(2,1)S(1)}, u32[]{:S(2)}, u32[]{:S(2)}) %all-to-all-start) | async-done | bytes 131104 | tf_op jit(solution)/shard_map/all_to_all | solution.py:12
  22.7 1.8 %collective-permute-start.5 = (bf16[64,1024]{1,0:T(8,128)(2,1)S(1)}, bf16[64,1024]{1,0:T(8,128)(2,1)S(1)}, u32[]{:S(2)}, u32[]{:S(2)}) collective-permute-start(bf16[64,1024]{1,0:T(8,128)(2,1)S(1)} %pad_maximum_fusion.2), channel_id=1, source_target_pairs={{0,6},{2,0},{4,2},{6,4},{1,7},{3,1},{5,3},{7,5},{8,14},{10,8},{12,... | collective-permute-start | bytes 393224 | tf_op jit(solution)/shard_map/ppermute | solution.py:17
  24.5 2.1 %collective-permute-start.4 = (bf16[64,1024]{1,0:T(8,128)(2,1)S(1)}, bf16[64,1024]{1,0:T(8,128)(2,1)S(1)}, u32[]{:S(2)}, u32[]{:S(2)}) collective-permute-start(bf16[64,1024]{1,0:T(8,128)(2,1)S(1)} %pad_maximum_fusion.2), channel_id=1, source_target_pairs={{0,4},{2,6},{4,0},{6,2},{1,5},{3,7},{5,1},{7,3},{8,12},{10,14},{12... | collective-permute-start | bytes 393224 | tf_op jit(solution)/shard_map/ppermute | solution.py:17
  26.6 1.5 %collective-permute-start.3 = (bf16[64,1024]{1,0:T(8,128)(2,1)S(1)}, bf16[64,1024]{1,0:T(8,128)(2,1)S(1)}, u32[]{:S(2)}, u32[]{:S(2)}) collective-permute-start(bf16[64,1024]{1,0:T(8,128)(2,1)S(1)} %pad_maximum_fusion.2), channel_id=1, source_target_pairs={{0,2},{2,4},{4,6},{6,0},{1,3},{3,5},{5,7},{7,1},{8,10},{10,12},{12... | collective-permute-start | bytes 393224 | tf_op jit(solution)/shard_map/ppermute | solution.py:17
  28.1 2.0 %collective-permute-start.7 = (bf16[256,1024]{1,0:T(8,128)(2,1)S(1)}, bf16[256,1024]{1,0:T(8,128)(2,1)S(1)}, u32[]{:S(2)}, u32[]{:S(2)}) collective-permute-start(bf16[256,1024]{1,0:T(8,128)(2,1)S(1)} %copy-done.1), channel_id=1, source_target_pairs={{0,64},{64,128},{128,192},{192,0},{1,65},{65,129},{129,193},{193,1... | collective-permute-start | bytes 1572872 | tf_op jit(solution)/shard_map/ppermute | solution.py:17
  33.8 8.2 %collective-permute-done.7 = bf16[256,1024]{1,0:T(8,128)(2,1)S(1)} collective-permute-done((bf16[256,1024]{1,0:T(8,128)(2,1)S(1)}, bf16[256,1024]{1,0:T(8,128)(2,1)S(1)}, u32[]{:S(2)}, u32[]{:S(2)}) %collective-permute-start.7) | collective-permute-done | bytes 524320 | tf_op jit(solution)/shard_map/ppermute | solution.py:17
  43.4 2.6 %collective-permute-start.10 = (bf16[128,1024]{1,0:T(8,128)(2,1)S(1)}, bf16[128,1024]{1,0:T(8,128)(2,1)S(1)}, u32[]{:S(2)}, u32[]{:S(2)}) collective-permute-start(bf16[128,1024]{1,0:T(8,128)(2,1)S(1)} %slice.128), channel_id=1, source_target_pairs={{0,192},{64,0},{128,64},{192,128},{1,193},{65,1},{129,65},{193,129... | collective-permute-start | bytes 786440 | tf_op jit(solution)/shard_map/ppermute | solution.py:17
  46.2 4.3 %collective-permute-done.8 = bf16[128,1024]{1,0:T(8,128)(2,1)S(1)} collective-permute-done((bf16[128,1024]{1,0:T(8,128)(2,1)}, bf16[128,1024]{1,0:T(8,128)(2,1)S(1)}, u32[]{:S(2)}, u32[]{:S(2)}) %collective-permute-start.8) | collective-permute-done | bytes 262176 | tf_op jit(solution)/shard_map/ppermute | solution.py:17
  52.2 2.2 %convolution_convert_fusion = bf16[512,1024]{1,0:T(8,128)(2,1)} fusion(bf16[512,1024]{1,0:T(8,128)(2,1)S(1)} %bitcast.112, bf16[1024,1024]{1,0:T(8,128)(2,1)S(1)} %constant_dynamic-update-slice_fusion), kind=kOutput, calls=%fused_computation | convolution fusion | flops 1074266112 | bytes 4194304 | tf_op jit(solution)/shard_map/dot_general | solution.py:52
  54.5 8.5 %all-to-all-start.1 = ((bf16[8,2,4,8,1024]{4,3,2,1,0:T(8,128)(2,1)}), bf16[8,2,4,8,1024]{4,3,2,1,0:T(8,128)(2,1)S(1)}, u32[]{:S(2)}, u32[]{:S(2)}) async-start(bf16[8,2,4,8,1024]{4,3,2,1,0:T(8,128)(2,1)} %bitcast.20), calls=%async_computation.1 | async-start | bytes 2097152 | tf_op jit(solution)/shard_map/all_to_all | solution.py:12
  63.0 8.3 %all-gather.2.cloned.1.call-done = bf16[512,1024]{1,0:T(8,128)(2,1)} async-done(((bf16[64,1024]{1,0:T(8,128)(2,1)}), bf16[512,1024]{1,0:T(8,128)(2,1)}) %all-gather.2.cloned.1.call-update) | async-done | bytes 1048592 | tf_op jit(solution)/shard_map/all_gather | solution.py:44
  71.3 3.3 %fusion.21 = f32[512,1024]{1,0:T(8,128)S(1)} fusion(bf16[512,1024]{1,0:T(8,128)(2,1)} %all-gather.2.cloned.1.call-done, bf16[1024,1024]{1,0:T(8,128)(2,1)} %copy-done.5), kind=kOutput, calls=%fused_computation.61 | convolution fusion | flops 1073741824 | bytes 5242880 | tf_op jit(solution)/shard_map/dot_general | solution.py:57
  76.3 2.4 %collective-permute-start.18 = (bf16[128,1024]{1,0:T(8,128)(2,1)S(1)}, bf16[128,1024]{1,0:T(8,128)(2,1)S(1)}, u32[]{:S(2)}, u32[]{:S(2)}) collective-permute-start(bf16[128,1024]{1,0:T(8,128)(2,1)S(1)} %get-tuple-element.51), channel_id=1, source_target_pairs={{0,192},{64,0},{128,64},{192,128},{1,193},{65,1},{129,65},{193,129... | collective-permute-start | bytes 786440 | tf_op jit(solution)/shard_map/ppermute | solution.py:17
  80.7 1.7 %collective-permute-start.14 = (bf16[8,8,1024]{2,1,0:T(8,128)(2,1)S(1)}, bf16[8,8,1024]{2,1,0:T(8,128)(2,1)S(1)}, u32[]{:S(2)}, u32[]{:S(2)}) collective-permute-start(bf16[8,8,1024]{2,1,0:T(8,128)(2,1)S(1)} %get-tuple-element.54), channel_id=1, source_target_pairs={{0,2},{2,4},{4,6},{6,0},{1,3},{3,5},{5,7},{7,1},{8,10},{10,12},{12... | collective-permute-start | bytes 393224 | tf_op jit(solution)/shard_map/ppermute | solution.py:17
  83.4 1.9 %collective-permute-done.18 = bf16[128,1024]{1,0:T(8,128)(2,1)S(1)} collective-permute-done((bf16[128,1024]{1,0:T(8,128)(2,1)S(1)}, bf16[128,1024]{1,0:T(8,128)(2,1)S(1)}, u32[]{:S(2)}, u32[]{:S(2)}) %collective-permute-start.18) | collective-permute-done | bytes 262176 | tf_op jit(solution)/shard_map/ppermute | solution.py:17
  85.3 3.0 %collective-permute-done.20 = bf16[128,1024]{1,0:T(8,128)(2,1)S(1)} collective-permute-done((bf16[128,1024]{1,0:T(8,128)(2,1)S(1)}, bf16[128,1024]{1,0:T(8,128)(2,1)S(1)}, u32[]{:S(2)}, u32[]{:S(2)}) %collective-permute-start.20) | collective-permute-done | bytes 262176 | tf_op jit(solution)/shard_map/ppermute | solution.py:17
  89.7 1.6 %collective-permute-start.21 = (bf16[2,128,1024]{2,1,0:T(8,128)(2,1)}, bf16[2,128,1024]{2,1,0:T(8,128)(2,1)S(1)}, u32[]{:S(2)}, u32[]{:S(2)}) collective-permute-start(bf16[2,128,1024]{2,1,0:T(8,128)(2,1)} %get-tuple-element.48), channel_id=1, source_target_pairs={{0,64},{64,128},{128,192},{192,0},{1,65},{65,129},{129,193},{193,1... | collective-permute-start | bytes 1572872 | tf_op jit(solution)/shard_map/ppermute | solution.py:17
  92.1 3.1 %collective-permute-start.16 = (f32[64,256]{1,0:T(8,128)}, f32[64,256]{1,0:T(8,128)}, u32[]{:S(2)}, u32[]{:S(2)}) collective-permute-start(f32[64,256]{1,0:T(8,128)} %get-tuple-element.59), channel_id=1, source_target_pairs={{0,128},{64,192},{128,0},{192,64},{1,129},{65,193},{129,1},{193,65... | collective-permute-start | bytes 196616 | tf_op jit(solution)/shard_map/ppermute | solution.py:17
  97.7 6.3 %all-to-all-start.2 = ((bf16[8,8,1024]{2,1,0:T(8,128)(2,1)}), bf16[8,8,1024]{2,1,0:T(8,128)(2,1)S(1)}, u32[]{:S(2)}, u32[]{:S(2)}) async-start(bf16[8,8,1024]{2,1,0:T(8,128)(2,1)} %bitcast.22), calls=%async_computation.2 | async-start | bytes 262144 | tf_op jit(solution)/shard_map/all_to_all | solution.py:12
  104.0 1.6 %collective-permute-done.15 = f32[64,256]{1,0:T(8,128)} collective-permute-done((f32[64,256]{1,0:T(8,128)}, f32[64,256]{1,0:T(8,128)}, u32[]{:S(2)}, u32[]{:S(2)}) %collective-permute-start.15) | collective-permute-done | bytes 65568 | tf_op jit(solution)/shard_map/ppermute | solution.py:17
  105.6 1.5 %bitcast_dynamic-update-slice_fusion.3 = f32[7,64,256]{2,1,0:T(8,128)} fusion(f32[7,64,256]{2,1,0:T(8,128)} %fusion.13, f32[64,256]{1,0:T(8,128)} %collective-permute-done.15), kind=kLoop, calls=%fused_computation.40 | loop fusion | bytes 131072
  108.6 1.5 %bitcast_dynamic-update-slice_fusion = f32[7,64,256]{2,1,0:T(8,128)} fusion(f32[7,64,256]{2,1,0:T(8,128)} %bitcast_dynamic-update-slice_fusion.1, f32[64,256]{1,0:T(8,128)} %collective-permute-done.17), kind=kLoop, calls=%fused_computation.37 | loop fusion | bytes 131072
  (88 shorter events, 28.9 us)
Async XLA Ops:
  9.0 9.5 %collective-permute-start.2 = (bf16[64,256]{1,0:T(8,128)(2,1)S(1)}, bf16[64,256]{1,0:T(8,128)(2,1)S(1)}, u32[]{:S(2)}, u32[]{:S(2)}) collective-permute-start(bf16[64,256]{1,0:T(8,128)(2,1)S(1)} %get-tuple-element.62), channel_id=1, source_target_pairs={{0,192},{64,0},{128,64},{192,128},{1,193},{65,1},{129,65},{193,129... | collective-permute-start | bytes 98312 | tf_op jit(solution)/shard_map/ppermute | solution.py:17
  12.1 6.4 %collective-permute-start.1 = (bf16[64,256]{1,0:T(8,128)(2,1)S(1)}, bf16[64,256]{1,0:T(8,128)(2,1)S(1)}, u32[]{:S(2)}, u32[]{:S(2)}) collective-permute-start(bf16[64,256]{1,0:T(8,128)(2,1)S(1)} %get-tuple-element.63), channel_id=1, source_target_pairs={{0,128},{64,192},{128,0},{192,64},{1,129},{65,193},{129,1},{193,65... | collective-permute-start | bytes 98312 | tf_op jit(solution)/shard_map/ppermute | solution.py:17
  13.7 8.2 %all-to-all-start = ((bf16[8,8,1024]{2,1,0:T(8,128)(2,1)}), bf16[8,8,1024]{2,1,0:T(8,128)(2,1)S(1)}, u32[]{:S(2)}, u32[]{:S(2)}) async-start(bf16[8,8,1024]{2,1,0:T(8,128)(2,1)} %bitcast.130), calls=%async_computation | async-start | bytes 262144 | tf_op jit(solution)/shard_map/all_to_all | solution.py:12
  18.5 52.8 %all-gather.2.cloned.1.call-start = ((), (), s32[]{:S(2)}) async-start(), calls=%async_computation.3 | async-start | bytes 1179648 | tf_op jit(solution)/shard_map/all_gather | solution.py:44
  22.7 8.7 %collective-permute-start.5 = (bf16[64,1024]{1,0:T(8,128)(2,1)S(1)}, bf16[64,1024]{1,0:T(8,128)(2,1)S(1)}, u32[]{:S(2)}, u32[]{:S(2)}) collective-permute-start(bf16[64,1024]{1,0:T(8,128)(2,1)S(1)} %pad_maximum_fusion.2), channel_id=1, source_target_pairs={{0,6},{2,0},{4,2},{6,4},{1,7},{3,1},{5,3},{7,5},{8,14},{10,8},{12,... | collective-permute-start | bytes 393224 | tf_op jit(solution)/shard_map/ppermute | solution.py:17
  24.5 7.7 %collective-permute-start.4 = (bf16[64,1024]{1,0:T(8,128)(2,1)S(1)}, bf16[64,1024]{1,0:T(8,128)(2,1)S(1)}, u32[]{:S(2)}, u32[]{:S(2)}) collective-permute-start(bf16[64,1024]{1,0:T(8,128)(2,1)S(1)} %pad_maximum_fusion.2), channel_id=1, source_target_pairs={{0,4},{2,6},{4,0},{6,2},{1,5},{3,7},{5,1},{7,3},{8,12},{10,14},{12... | collective-permute-start | bytes 393224 | tf_op jit(solution)/shard_map/ppermute | solution.py:17
  26.6 7.0 %collective-permute-start.3 = (bf16[64,1024]{1,0:T(8,128)(2,1)S(1)}, bf16[64,1024]{1,0:T(8,128)(2,1)S(1)}, u32[]{:S(2)}, u32[]{:S(2)}) collective-permute-start(bf16[64,1024]{1,0:T(8,128)(2,1)S(1)} %pad_maximum_fusion.2), channel_id=1, source_target_pairs={{0,2},{2,4},{4,6},{6,0},{1,3},{3,5},{5,7},{7,1},{8,10},{10,12},{12... | collective-permute-start | bytes 393224 | tf_op jit(solution)/shard_map/ppermute | solution.py:17
  28.1 13.9 %collective-permute-start.7 = (bf16[256,1024]{1,0:T(8,128)(2,1)S(1)}, bf16[256,1024]{1,0:T(8,128)(2,1)S(1)}, u32[]{:S(2)}, u32[]{:S(2)}) collective-permute-start(bf16[256,1024]{1,0:T(8,128)(2,1)S(1)} %copy-done.1), channel_id=1, source_target_pairs={{0,64},{64,128},{128,192},{192,0},{1,65},{65,129},{129,193},{193,1... | collective-permute-start | bytes 1572872 | tf_op jit(solution)/shard_map/ppermute | solution.py:17
  30.0 13.4 %collective-permute-start.9 = (bf16[256,1024]{1,0:T(8,128)(2,1)S(1)}, bf16[256,1024]{1,0:T(8,128)(2,1)S(1)}, u32[]{:S(2)}, u32[]{:S(2)}) collective-permute-start(bf16[256,1024]{1,0:T(8,128)(2,1)S(1)} %copy-done.1), channel_id=1, source_target_pairs={{0,192},{64,0},{128,64},{192,128},{1,193},{65,1},{129,65},{193,129... | collective-permute-start | bytes 1572872 | tf_op jit(solution)/shard_map/ppermute | solution.py:17
  33.7 12.4 %collective-permute-start.6 = (bf16[4,64,1024]{2,1,0:T(8,128)(2,1)S(1)}, bf16[4,64,1024]{2,1,0:T(8,128)(2,1)S(1)}, u32[]{:S(2)}, u32[]{:S(2)}) collective-permute-start(bf16[4,64,1024]{2,1,0:T(8,128)(2,1)S(1)} %get-tuple-element.57), channel_id=1, source_target_pairs={{0,1},{1,0},{2,3},{3,2},{4,5},{5,4},{6,7},{7,6},{8,9},{9,8},{10,11... | collective-permute-start | bytes 1572872 | tf_op jit(solution)/shard_map/ppermute | solution.py:17
  42.7 7.8 %collective-permute-start.8 = (bf16[128,1024]{1,0:T(8,128)(2,1)}, bf16[128,1024]{1,0:T(8,128)(2,1)S(1)}, u32[]{:S(2)}, u32[]{:S(2)}) collective-permute-start(bf16[128,1024]{1,0:T(8,128)(2,1)} %slice.127), channel_id=1, source_target_pairs={{0,64},{64,128},{128,192},{192,0},{1,65},{65,129},{129,193},{193,1... | collective-permute-start | bytes 786440 | tf_op jit(solution)/shard_map/ppermute | solution.py:17
  43.4 7.1 %collective-permute-start.10 = (bf16[128,1024]{1,0:T(8,128)(2,1)S(1)}, bf16[128,1024]{1,0:T(8,128)(2,1)S(1)}, u32[]{:S(2)}, u32[]{:S(2)}) collective-permute-start(bf16[128,1024]{1,0:T(8,128)(2,1)S(1)} %slice.128), channel_id=1, source_target_pairs={{0,192},{64,0},{128,64},{192,128},{1,193},{65,1},{129,65},{193,129... | collective-permute-start | bytes 786440 | tf_op jit(solution)/shard_map/ppermute | solution.py:17
  54.5 42.3 %all-to-all-start.1 = ((bf16[8,2,4,8,1024]{4,3,2,1,0:T(8,128)(2,1)}), bf16[8,2,4,8,1024]{4,3,2,1,0:T(8,128)(2,1)S(1)}, u32[]{:S(2)}, u32[]{:S(2)}) async-start(bf16[8,2,4,8,1024]{4,3,2,1,0:T(8,128)(2,1)} %bitcast.20), calls=%async_computation.1 | async-start | bytes 2097152 | tf_op jit(solution)/shard_map/all_to_all | solution.py:12
  76.3 9.0 %collective-permute-start.18 = (bf16[128,1024]{1,0:T(8,128)(2,1)S(1)}, bf16[128,1024]{1,0:T(8,128)(2,1)S(1)}, u32[]{:S(2)}, u32[]{:S(2)}) collective-permute-start(bf16[128,1024]{1,0:T(8,128)(2,1)S(1)} %get-tuple-element.51), channel_id=1, source_target_pairs={{0,192},{64,0},{128,64},{192,128},{1,193},{65,1},{129,65},{193,129... | collective-permute-start | bytes 786440 | tf_op jit(solution)/shard_map/ppermute | solution.py:17
  78.7 9.6 %collective-permute-start.20 = (bf16[128,1024]{1,0:T(8,128)(2,1)S(1)}, bf16[128,1024]{1,0:T(8,128)(2,1)S(1)}, u32[]{:S(2)}, u32[]{:S(2)}) collective-permute-start(bf16[128,1024]{1,0:T(8,128)(2,1)S(1)} %get-tuple-element.52), channel_id=1, source_target_pairs={{0,64},{64,128},{128,192},{192,0},{1,65},{65,129},{129,193},{193,1... | collective-permute-start | bytes 786440 | tf_op jit(solution)/shard_map/ppermute | solution.py:17
  80.3 11.1 %collective-permute-start.12 = (bf16[8,8,1024]{2,1,0:T(8,128)(2,1)S(1)}, bf16[8,8,1024]{2,1,0:T(8,128)(2,1)S(1)}, u32[]{:S(2)}, u32[]{:S(2)}) collective-permute-start(bf16[8,8,1024]{2,1,0:T(8,128)(2,1)S(1)} %get-tuple-element.53), channel_id=1, source_target_pairs={{0,6},{2,0},{4,2},{6,4},{1,7},{3,1},{5,3},{7,5},{8,14},{10,8},{12,... | collective-permute-start | bytes 393224 | tf_op jit(solution)/shard_map/ppermute | solution.py:17
  80.7 10.7 %collective-permute-start.14 = (bf16[8,8,1024]{2,1,0:T(8,128)(2,1)S(1)}, bf16[8,8,1024]{2,1,0:T(8,128)(2,1)S(1)}, u32[]{:S(2)}, u32[]{:S(2)}) collective-permute-start(bf16[8,8,1024]{2,1,0:T(8,128)(2,1)S(1)} %get-tuple-element.54), channel_id=1, source_target_pairs={{0,2},{2,4},{4,6},{6,0},{1,3},{3,5},{5,7},{7,1},{8,10},{10,12},{12... | collective-permute-start | bytes 393224 | tf_op jit(solution)/shard_map/ppermute | solution.py:17
  82.4 9.0 %collective-permute-start.13 = (bf16[8,8,1024]{2,1,0:T(8,128)(2,1)S(1)}, bf16[8,8,1024]{2,1,0:T(8,128)(2,1)S(1)}, u32[]{:S(2)}, u32[]{:S(2)}) collective-permute-start(bf16[8,8,1024]{2,1,0:T(8,128)(2,1)S(1)} %get-tuple-element.55), channel_id=1, source_target_pairs={{0,4},{2,6},{4,0},{6,2},{1,5},{3,7},{5,1},{7,3},{8,12},{10,14},{12... | collective-permute-start | bytes 393224 | tf_op jit(solution)/shard_map/ppermute | solution.py:17
  89.3 25.9 %collective-permute-start.19 = (bf16[2,128,1024]{2,1,0:T(8,128)(2,1)}, bf16[2,128,1024]{2,1,0:T(8,128)(2,1)S(1)}, u32[]{:S(2)}, u32[]{:S(2)}) collective-permute-start(bf16[2,128,1024]{2,1,0:T(8,128)(2,1)} %get-tuple-element.47), channel_id=1, source_target_pairs={{0,192},{64,0},{128,64},{192,128},{1,193},{65,1},{129,65},{193,129... | collective-permute-start | bytes 1572872 | tf_op jit(solution)/shard_map/ppermute | solution.py:17
  89.7 25.5 %collective-permute-start.21 = (bf16[2,128,1024]{2,1,0:T(8,128)(2,1)}, bf16[2,128,1024]{2,1,0:T(8,128)(2,1)S(1)}, u32[]{:S(2)}, u32[]{:S(2)}) collective-permute-start(bf16[2,128,1024]{2,1,0:T(8,128)(2,1)} %get-tuple-element.48), channel_id=1, source_target_pairs={{0,64},{64,128},{128,192},{192,0},{1,65},{65,129},{129,193},{193,1... | collective-permute-start | bytes 1572872 | tf_op jit(solution)/shard_map/ppermute | solution.py:17
  92.1 16.5 %collective-permute-start.17 = (f32[64,256]{1,0:T(8,128)}, f32[64,256]{1,0:T(8,128)}, u32[]{:S(2)}, u32[]{:S(2)}) collective-permute-start(f32[64,256]{1,0:T(8,128)} %get-tuple-element.58), channel_id=1, source_target_pairs={{0,64},{64,128},{128,192},{192,0},{1,65},{65,129},{129,193},{193,1... | collective-permute-start | bytes 196616 | tf_op jit(solution)/shard_map/ppermute | solution.py:17
  92.1 15.0 %collective-permute-start.16 = (f32[64,256]{1,0:T(8,128)}, f32[64,256]{1,0:T(8,128)}, u32[]{:S(2)}, u32[]{:S(2)}) collective-permute-start(f32[64,256]{1,0:T(8,128)} %get-tuple-element.59), channel_id=1, source_target_pairs={{0,128},{64,192},{128,0},{192,64},{1,129},{65,193},{129,1},{193,65... | collective-permute-start | bytes 196616 | tf_op jit(solution)/shard_map/ppermute | solution.py:17
  95.2 10.5 %collective-permute-start.15 = (f32[64,256]{1,0:T(8,128)}, f32[64,256]{1,0:T(8,128)}, u32[]{:S(2)}, u32[]{:S(2)}) collective-permute-start(f32[64,256]{1,0:T(8,128)} %get-tuple-element.60), channel_id=1, source_target_pairs={{0,192},{64,0},{128,64},{192,128},{1,193},{65,1},{129,65},{193,129... | collective-permute-start | bytes 196616 | tf_op jit(solution)/shard_map/ppermute | solution.py:17
  97.7 17.5 %all-to-all-start.2 = ((bf16[8,8,1024]{2,1,0:T(8,128)(2,1)}), bf16[8,8,1024]{2,1,0:T(8,128)(2,1)S(1)}, u32[]{:S(2)}, u32[]{:S(2)}) async-start(bf16[8,8,1024]{2,1,0:T(8,128)(2,1)} %bitcast.22), calls=%async_computation.2 | async-start | bytes 262144 | tf_op jit(solution)/shard_map/all_to_all | solution.py:12
  (8 other events, 44.9 us)
Sparse Core Ops, SparseCore 0:
  28.2 43.0 all-gather.1
where the time goes:
time: 125 us; the launch traced here: 124 us
  starting transfers between devices  48.2 us (39%)
  waiting for transfers between devices  33.1 us (26%)
  local copies, waits for them, and re-layouts  15.4 us (12%)
  between operations  14.4 us (12%)
  matrix products  6.85 us (5%)
  other arithmetic  5.94 us (5%)
    ppermute x22, starting transfers between devices, shift(): return lax.ppermute(v, axis, [(i, (i + s) % n) for i in range(n)])  28.7 us
    ppermute x22, waiting for transfers between devices, shift(): return lax.ppermute(v, axis, [(i, (i + s) % n) for i in range(n)])  21.4 us
    all_to_all x3, starting transfers between devices, exchange(): return lax.all_to_all(v, axes, split_axis=0, concat_axis=0, tiled=False)  19.5 us
    unnamed x23, local copies, waits for them, and re-layouts  9.32 us
    all_gather x1, waiting for transfers between devices, shards(): g = lax.all_gather(g, 'z', axis=0, tiled=True)  8.31 us
    all_to_all x3, waiting for transfers between devices, exchange(): return lax.all_to_all(v, axes, split_axis=0, concat_axis=0, tiled=False)  3.38 us
    dot_general x1, matrix products, shards(): lax.dot_general(g, w, (((1,), (1,)), ((), ())), preferred_element_type=F32)  3.28 us
  transfers between devices with their start and end apart: 26, of which 9 were waited for; matrix products, arithmetic and copies ran while one was open for 18% of the time, Pallas kernels for 0%

commit v1 on v0

--- a/solution.py
+++ b/solution.py
@@ -41,7 +41,7 @@
     a = [a[0]] + [shift(a[s], "y", s) for s in range(1, ny)]
     a = jnp.concatenate(a, axis=1)
     a, g = lax.optimization_barrier((a, g.reshape(nc * nx * j, n)))
-    g = lax.all_gather(g, "z", axis=0, tiled=True)
+    g = jnp.concatenate(lax.all_to_all(jnp.stack([g] * lax.axis_size("z")), "z", 0, 0), axis=0)
     a = jnp.stack([a] + [shift(a, "x", s) for s in range(1, nx)])
     a = jnp.stack([a, shift(a, "c", 1)])
     w1, w3 = (shift(w_out, "y", 1), shift(w_out, "y", -1))

time: 125 us -> 114 us (0.912)
  between operations: 14.4 us -> 0.95 us
  waiting for transfers between devices: 33.1 us -> 22.8 us
  starting transfers between devices: 48.2 us -> 55.5 us
  local copies, waits for them, and re-layouts: 15.4 us -> 19.9 us
  other arithmetic: 5.94 us -> 7.19 us
    all_to_all x0 -> x1, starting transfers between devices: none -> 8.47 us  [shards(): lax.all_to_all(jnp.stack([g] * lax.axis_size('z')), 'z', 0, 0)]
    all_gather x1 -> x0, waiting for transfers between devices: 8.31 us -> none  [shards(): g = lax.all_gather(g, 'z', axis=0, tiled=True)]
    unnamed x23 -> x15, local copies, waits for them, and re-layouts: 9.32 us -> 11.9 us
    ppermute x22, waiting for transfers between devices: 21.4 us -> 19.4 us  [shift(): return lax.ppermute(v, axis, [(i, (i + s) % n) for i in range(n)])]
    another operation x2, other arithmetic: 0.18 us -> 2.13 us  [shards(): a = jnp.stack([a, shift(a, 'c', 1)])]
    all_to_all x3, starting transfers between devices: 19.5 us -> 17.7 us  [exchange(): return lax.all_to_all(v, axes, split_axis=0, concat_axis=0, tiled=False)]
  transfers between devices with their start and end apart: 26 -> 26, of which waited for: 9 -> 7; matrix products, arithmetic and copies ran while one was open for 18% -> 25% of each run, Pallas kernels for 0% -> 0%
where the time goes in v1:
time: 114 us; the launch traced here: 113 us
  starting transfers between devices  55.5 us (49%)
  waiting for transfers between devices  22.8 us (20%)
  local copies, waits for them, and re-layouts  19.9 us (17%)
  other arithmetic  7.19 us (6%)
  matrix products  6.41 us (6%)
    ppermute x22, starting transfers between devices, shift(): return lax.ppermute(v, axis, [(i, (i + s) % n) for i in range(n)])  29.3 us
    ppermute x22, waiting for transfers between devices, shift(): return lax.ppermute(v, axis, [(i, (i + s) % n) for i in range(n)])  19.4 us
    all_to_all x3, starting transfers between devices, exchange(): return lax.all_to_all(v, axes, split_axis=0, concat_axis=0, tiled=False)  17.7 us
    unnamed x15, local copies, waits for them, and re-layouts  11.9 us
    all_to_all x1, starting transfers between devices, shards(): lax.all_to_all(jnp.stack([g] * lax.axis_size('z')), 'z', 0, 0)  8.47 us
    all_to_all x3, waiting for transfers between devices, exchange(): return lax.all_to_all(v, axes, split_axis=0, concat_axis=0, tiled=False)  3.39 us
    dot_general x1, matrix products, shards(): lax.dot_general(g, w, (((1,), (1,)), ((), ())), preferred_element_type=F32)  2.87 us
  transfers between devices with their start and end apart: 26, of which 7 were waited for; matrix products, arithmetic and copies ran while one was open for 25% of the time, Pallas kernels for 0%

profile of v1, /device:TPU:4, one launch (start us, length us, event | category | flops | bytes accessed | tf_op | source)
XLA Modules:
  0.0 112.7 jit_solution(15040831009170446025)
XLA Ops:
  2.4 3.1 %collective-permute-start.2 = (bf16[64,256]{1,0:T(8,128)(2,1)S(1)}, bf16[64,256]{1,0:T(8,128)(2,1)S(1)}, u32[]{:S(2)}, u32[]{:S(2)}) collective-permute-start(bf16[64,256]{1,0:T(8,128)(2,1)S(1)} %get-tuple-element.62), channel_id=1, source_target_pairs={{0,192},{64,0},{128,64},{192,128},{1,193},{65,1},{129,65},{193,129... | collective-permute-start | bytes 98312 | tf_op jit(solution)/shard_map/ppermute | solution.py:17
  7.1 4.8 %all-to-all-start = ((bf16[8,8,1024]{2,1,0:T(8,128)(2,1)}), bf16[8,8,1024]{2,1,0:T(8,128)(2,1)S(1)}, u32[]{:S(2)}, u32[]{:S(2)}) async-start(bf16[8,8,1024]{2,1,0:T(8,128)(2,1)} %bitcast.137), calls=%async_computation | async-start | bytes 262144 | tf_op jit(solution)/shard_map/all_to_all | solution.py:12
  11.9 3.4 %all-to-all-done = bf16[8,8,1024]{2,1,0:T(8,128)(2,1)S(1)} async-done(((bf16[8,8,1024]{2,1,0:T(8,128)(2,1)}), bf16[8,8,1024]{2,1,0:T(8,128)(2,1)S(1)}, u32[]{:S(2)}, u32[]{:S(2)}) %all-to-all-start) | async-done | bytes 131104 | tf_op jit(solution)/shard_map/all_to_all | solution.py:12
  15.5 1.9 %collective-permute-start.5 = (bf16[64,1024]{1,0:T(8,128)(2,1)S(1)}, bf16[64,1024]{1,0:T(8,128)(2,1)S(1)}, u32[]{:S(2)}, u32[]{:S(2)}) collective-permute-start(bf16[64,1024]{1,0:T(8,128)(2,1)S(1)} %pad_maximum_fusion.2), channel_id=1, source_target_pairs={{0,6},{2,0},{4,2},{6,4},{1,7},{3,1},{5,3},{7,5},{8,14},{10,8},{12,... | collective-permute-start | bytes 393224 | tf_op jit(solution)/shard_map/ppermute | solution.py:17
  17.4 2.1 %collective-permute-start.4 = (bf16[64,1024]{1,0:T(8,128)(2,1)S(1)}, bf16[64,1024]{1,0:T(8,128)(2,1)S(1)}, u32[]{:S(2)}, u32[]{:S(2)}) collective-permute-start(bf16[64,1024]{1,0:T(8,128)(2,1)S(1)} %pad_maximum_fusion.2), channel_id=1, source_target_pairs={{0,4},{2,6},{4,0},{6,2},{1,5},{3,7},{5,1},{7,3},{8,12},{10,14},{12... | collective-permute-start | bytes 393224 | tf_op jit(solution)/shard_map/ppermute | solution.py:17
  22.0 8.5 %all-to-all-start.3 = ((bf16[8,64,1024]{2,1,0:T(8,128)(2,1)}), bf16[8,64,1024]{2,1,0:T(8,128)(2,1)S(1)}, u32[]{:S(2)}, u32[]{:S(2)}) async-start(bf16[8,64,1024]{2,1,0:T(8,128)(2,1)} %stack.61), calls=%async_computation.3 | async-start | bytes 2097152 | tf_op jit(solution)/shard_map/all_to_all | solution.py:44
  30.5 1.9 %collective-permute-start.7 = (bf16[256,1024]{1,0:T(8,128)(2,1)}, bf16[256,1024]{1,0:T(8,128)(2,1)S(1)}, u32[]{:S(2)}, u32[]{:S(2)}) collective-permute-start(bf16[256,1024]{1,0:T(8,128)(2,1)} %param.12), channel_id=1, source_target_pairs={{0,64},{64,128},{128,192},{192,0},{1,65},{65,129},{129,193},{193,1... | collective-permute-start | bytes 1572872 | tf_op jit(solution)/shard_map/ppermute | solution.py:17
  35.5 8.8 %collective-permute-done.7 = bf16[256,1024]{1,0:T(8,128)(2,1)S(1)} collective-permute-done((bf16[256,1024]{1,0:T(8,128)(2,1)}, bf16[256,1024]{1,0:T(8,128)(2,1)S(1)}, u32[]{:S(2)}, u32[]{:S(2)}) %collective-permute-start.7) | collective-permute-done | bytes 524320 | tf_op jit(solution)/shard_map/ppermute | solution.py:17
  46.4 2.6 %collective-permute-start.10 = (bf16[128,1024]{1,0:T(8,128)(2,1)}, bf16[128,1024]{1,0:T(8,128)(2,1)}, u32[]{:S(2)}, u32[]{:S(2)}) collective-permute-start(bf16[128,1024]{1,0:T(8,128)(2,1)} %slice.128), channel_id=1, source_target_pairs={{0,192},{64,0},{128,64},{192,128},{1,193},{65,1},{129,65},{193,129... | collective-permute-start | bytes 786440 | tf_op jit(solution)/shard_map/ppermute | solution.py:17
  50.1 2.7 %collective-permute-done.8 = bf16[128,1024]{1,0:T(8,128)(2,1)S(1)} collective-permute-done((bf16[128,1024]{1,0:T(8,128)(2,1)}, bf16[128,1024]{1,0:T(8,128)(2,1)S(1)}, u32[]{:S(2)}, u32[]{:S(2)}) %collective-permute-start.8) | collective-permute-done | bytes 262176 | tf_op jit(solution)/shard_map/ppermute | solution.py:17
  56.8 2.3 %convolution_convert_fusion = bf16[512,1024]{1,0:T(8,128)(2,1)} fusion(bf16[512,1024]{1,0:T(8,128)(2,1)S(1)} %bitcast.119, bf16[1024,1024]{1,0:T(8,128)(2,1)S(1)} %constant_dynamic-update-slice_fusion), kind=kOutput, calls=%fused_computation.3 | convolution fusion | flops 1074266112 | bytes 4194304 | tf_op jit(solution)/shard_map/dot_general | solution.py:52
  59.0 6.9 %all-to-all-start.1 = ((bf16[8,2,4,8,1024]{4,3,2,1,0:T(8,128)(2,1)}), bf16[8,2,4,8,1024]{4,3,2,1,0:T(8,128)(2,1)S(1)}, u32[]{:S(2)}, u32[]{:S(2)}) async-start(bf16[8,2,4,8,1024]{4,3,2,1,0:T(8,128)(2,1)} %bitcast.127), calls=%async_computation.1 | async-start | bytes 2097152 | tf_op jit(solution)/shard_map/all_to_all | solution.py:12
  65.9 2.9 %fusion.2 = f32[2,4,8,8,1024]{4,3,1,0,2:T(8,128)S(1)} fusion(bf16[8,2,4,8,1024]{4,3,2,1,0:T(8,128)(2,1)S(1)} %bitcast.123, bf16[1024,1024]{1,0:T(8,128)(2,1)} %copy-done.1), kind=kOutput, calls=%fused_computation.2 | convolution fusion | flops 1073741824 | bytes 5242880 | tf_op jit(solution)/shard_map/dot_general | solution.py:57
  70.5 3.8 %collective-permute-start.18 = (bf16[128,1024]{1,0:T(8,128)(2,1)S(1)}, bf16[128,1024]{1,0:T(8,128)(2,1)S(1)}, u32[]{:S(2)}, u32[]{:S(2)}) collective-permute-start(bf16[128,1024]{1,0:T(8,128)(2,1)S(1)} %get-tuple-element.51), channel_id=1, source_target_pairs={{0,192},{64,0},{128,64},{192,128},{1,193},{65,1},{129,65},{193,129... | collective-permute-start | bytes 786440 | tf_op jit(solution)/shard_map/ppermute | solution.py:17
  80.5 3.4 %collective-permute-done.20 = bf16[128,1024]{1,0:T(8,128)(2,1)S(1)} collective-permute-done((bf16[128,1024]{1,0:T(8,128)(2,1)S(1)}, bf16[128,1024]{1,0:T(8,128)(2,1)S(1)}, u32[]{:S(2)}, u32[]{:S(2)}) %collective-permute-start.20) | collective-permute-done | bytes 262176 | tf_op jit(solution)/shard_map/ppermute | solution.py:17
  85.2 1.7 %collective-permute-start.21 = (bf16[2,128,1024]{2,1,0:T(8,128)(2,1)}, bf16[2,128,1024]{2,1,0:T(8,128)(2,1)S(1)}, u32[]{:S(2)}, u32[]{:S(2)}) collective-permute-start(bf16[2,128,1024]{2,1,0:T(8,128)(2,1)} %get-tuple-element.48), channel_id=1, source_target_pairs={{0,64},{64,128},{128,192},{192,0},{1,65},{65,129},{129,193},{193,1... | collective-permute-start | bytes 1572872 | tf_op jit(solution)/shard_map/ppermute | solution.py:17
  87.7 3.0 %collective-permute-start.16 = (f32[64,256]{1,0:T(8,128)}, f32[64,256]{1,0:T(8,128)}, u32[]{:S(2)}, u32[]{:S(2)}) collective-permute-start(f32[64,256]{1,0:T(8,128)} %get-tuple-element.59), channel_id=1, source_target_pairs={{0,128},{64,192},{128,0},{192,64},{1,129},{65,193},{129,1},{193,65... | collective-permute-start | bytes 196616 | tf_op jit(solution)/shard_map/ppermute | solution.py:17
  92.5 6.0 %all-to-all-start.2 = ((bf16[8,8,1024]{2,1,0:T(8,128)(2,1)}), bf16[8,8,1024]{2,1,0:T(8,128)(2,1)S(1)}, u32[]{:S(2)}, u32[]{:S(2)}) async-start(bf16[8,8,1024]{2,1,0:T(8,128)(2,1)} %bitcast.22), calls=%async_computation.2 | async-start | bytes 262144 | tf_op jit(solution)/shard_map/all_to_all | solution.py:12
  98.5 2.7 %collective-permute-done.15 = f32[64,256]{1,0:T(8,128)} collective-permute-done((f32[64,256]{1,0:T(8,128)}, f32[64,256]{1,0:T(8,128)}, u32[]{:S(2)}, u32[]{:S(2)}) %collective-permute-start.15) | collective-permute-done | bytes 65568 | tf_op jit(solution)/shard_map/ppermute | solution.py:17
  101.2 1.5 %bitcast_dynamic-update-slice_fusion.3 = f32[7,64,256]{2,1,0:T(8,128)} fusion(f32[7,64,256]{2,1,0:T(8,128)} %fusion.18, f32[64,256]{1,0:T(8,128)} %collective-permute-done.15), kind=kLoop, calls=%fused_computation.43 | loop fusion | bytes 131072
  102.7 1.5 %bitcast_dynamic-update-slice_fusion.1 = f32[7,64,256]{2,1,0:T(8,128)} fusion(f32[7,64,256]{2,1,0:T(8,128)} %bitcast_dynamic-update-slice_fusion.3, f32[64,256]{1,0:T(8,128)} %collective-permute-done.16), kind=kLoop, calls=%fused_computation.41 | loop fusion | bytes 131072
  104.2 1.5 %bitcast_dynamic-update-slice_fusion = f32[7,64,256]{2,1,0:T(8,128)} fusion(f32[7,64,256]{2,1,0:T(8,128)} %bitcast_dynamic-update-slice_fusion.1, f32[64,256]{1,0:T(8,128)} %collective-permute-done.17), kind=kLoop, calls=%fused_computation.40 | loop fusion | bytes 131072
  106.3 1.5 %bitcast_dynamic-update-slice_fusion.4 = f32[7,64,256]{2,1,0:T(8,128)} fusion(f32[7,64,256]{2,1,0:T(8,128)} %fusion.19, f32[64,256]{1,0:T(8,128)} %collective-permute-done.15), kind=kLoop, calls=%fused_computation.44 | loop fusion | bytes 131072
  107.8 1.5 %bitcast_dynamic-update-slice_fusion.2 = f32[7,64,256]{2,1,0:T(8,128)} fusion(f32[7,64,256]{2,1,0:T(8,128)} %bitcast_dynamic-update-slice_fusion.4, f32[64,256]{1,0:T(8,128)} %collective-permute-done.16), kind=kLoop, calls=%fused_computation.42 | loop fusion | bytes 131072 | tf_op jit(solution)/shard_map/stack | solution.py:66
  (80 shorter events, 32.1 us)
Async XLA Ops:
  2.4 9.5 %collective-permute-start.2 = (bf16[64,256]{1,0:T(8,128)(2,1)S(1)}, bf16[64,256]{1,0:T(8,128)(2,1)S(1)}, u32[]{:S(2)}, u32[]{:S(2)}) collective-permute-start(bf16[64,256]{1,0:T(8,128)(2,1)S(1)} %get-tuple-element.62), channel_id=1, source_target_pairs={{0,192},{64,0},{128,64},{192,128},{1,193},{65,1},{129,65},{193,129... | collective-permute-start | bytes 98312 | tf_op jit(solution)/shard_map/ppermute | solution.py:17
  7.1 8.2 %all-to-all-start = ((bf16[8,8,1024]{2,1,0:T(8,128)(2,1)}), bf16[8,8,1024]{2,1,0:T(8,128)(2,1)S(1)}, u32[]{:S(2)}, u32[]{:S(2)}) async-start(bf16[8,8,1024]{2,1,0:T(8,128)(2,1)} %bitcast.137), calls=%async_computation | async-start | bytes 262144 | tf_op jit(solution)/shard_map/all_to_all | solution.py:12
  15.5 18.2 %collective-permute-start.5 = (bf16[64,1024]{1,0:T(8,128)(2,1)S(1)}, bf16[64,1024]{1,0:T(8,128)(2,1)S(1)}, u32[]{:S(2)}, u32[]{:S(2)}) collective-permute-start(bf16[64,1024]{1,0:T(8,128)(2,1)S(1)} %pad_maximum_fusion.2), channel_id=1, source_target_pairs={{0,6},{2,0},{4,2},{6,4},{1,7},{3,1},{5,3},{7,5},{8,14},{10,8},{12,... | collective-permute-start | bytes 393224 | tf_op jit(solution)/shard_map/ppermute | solution.py:17
  17.4 16.4 %collective-permute-start.4 = (bf16[64,1024]{1,0:T(8,128)(2,1)S(1)}, bf16[64,1024]{1,0:T(8,128)(2,1)S(1)}, u32[]{:S(2)}, u32[]{:S(2)}) collective-permute-start(bf16[64,1024]{1,0:T(8,128)(2,1)S(1)} %pad_maximum_fusion.2), channel_id=1, source_target_pairs={{0,4},{2,6},{4,0},{6,2},{1,5},{3,7},{5,1},{7,3},{8,12},{10,14},{12... | collective-permute-start | bytes 393224 | tf_op jit(solution)/shard_map/ppermute | solution.py:17
  19.4 14.3 %collective-permute-start.3 = (bf16[64,1024]{1,0:T(8,128)(2,1)S(1)}, bf16[64,1024]{1,0:T(8,128)(2,1)S(1)}, u32[]{:S(2)}, u32[]{:S(2)}) collective-permute-start(bf16[64,1024]{1,0:T(8,128)(2,1)S(1)} %pad_maximum_fusion.2), channel_id=1, source_target_pairs={{0,2},{2,4},{4,6},{6,0},{1,3},{3,5},{5,7},{7,1},{8,10},{10,12},{12... | collective-permute-start | bytes 393224 | tf_op jit(solution)/shard_map/ppermute | solution.py:17
  22.0 37.0 %all-to-all-start.3 = ((bf16[8,64,1024]{2,1,0:T(8,128)(2,1)}), bf16[8,64,1024]{2,1,0:T(8,128)(2,1)S(1)}, u32[]{:S(2)}, u32[]{:S(2)}) async-start(bf16[8,64,1024]{2,1,0:T(8,128)(2,1)} %stack.61), calls=%async_computation.3 | async-start | bytes 2097152 | tf_op jit(solution)/shard_map/all_to_all | solution.py:44
  30.5 13.8 %collective-permute-start.7 = (bf16[256,1024]{1,0:T(8,128)(2,1)}, bf16[256,1024]{1,0:T(8,128)(2,1)S(1)}, u32[]{:S(2)}, u32[]{:S(2)}) collective-permute-start(bf16[256,1024]{1,0:T(8,128)(2,1)} %param.12), channel_id=1, source_target_pairs={{0,64},{64,128},{128,192},{192,0},{1,65},{65,129},{129,193},{193,1... | collective-permute-start | bytes 1572872 | tf_op jit(solution)/shard_map/ppermute | solution.py:17
  32.3 13.3 %collective-permute-start.9 = (bf16[256,1024]{1,0:T(8,128)(2,1)}, bf16[256,1024]{1,0:T(8,128)(2,1)S(1)}, u32[]{:S(2)}, u32[]{:S(2)}) collective-permute-start(bf16[256,1024]{1,0:T(8,128)(2,1)} %param.12), channel_id=1, source_target_pairs={{0,192},{64,0},{128,64},{192,128},{1,193},{65,1},{129,65},{193,129... | collective-permute-start | bytes 1572872 | tf_op jit(solution)/shard_map/ppermute | solution.py:17
  35.4 13.6 %collective-permute-start.6 = (bf16[4,64,1024]{2,1,0:T(8,128)(2,1)S(1)}, bf16[4,64,1024]{2,1,0:T(8,128)(2,1)}, u32[]{:S(2)}, u32[]{:S(2)}) collective-permute-start(bf16[4,64,1024]{2,1,0:T(8,128)(2,1)S(1)} %get-tuple-element.57), channel_id=1, source_target_pairs={{0,1},{1,0},{2,3},{3,2},{4,5},{5,4},{6,7},{7,6},{8,9},{9,8},{10,11... | collective-permute-start | bytes 1572872 | tf_op jit(solution)/shard_map/ppermute | solution.py:17
  45.0 7.8 %collective-permute-start.8 = (bf16[128,1024]{1,0:T(8,128)(2,1)}, bf16[128,1024]{1,0:T(8,128)(2,1)S(1)}, u32[]{:S(2)}, u32[]{:S(2)}) collective-permute-start(bf16[128,1024]{1,0:T(8,128)(2,1)} %slice.127), channel_id=1, source_target_pairs={{0,64},{64,128},{128,192},{192,0},{1,65},{65,129},{129,193},{193,1... | collective-permute-start | bytes 786440 | tf_op jit(solution)/shard_map/ppermute | solution.py:17
  46.4 6.8 %collective-permute-start.10 = (bf16[128,1024]{1,0:T(8,128)(2,1)}, bf16[128,1024]{1,0:T(8,128)(2,1)}, u32[]{:S(2)}, u32[]{:S(2)}) collective-permute-start(bf16[128,1024]{1,0:T(8,128)(2,1)} %slice.128), channel_id=1, source_target_pairs={{0,192},{64,0},{128,64},{192,128},{1,193},{65,1},{129,65},{193,129... | collective-permute-start | bytes 786440 | tf_op jit(solution)/shard_map/ppermute | solution.py:17
  59.0 32.5 %all-to-all-start.1 = ((bf16[8,2,4,8,1024]{4,3,2,1,0:T(8,128)(2,1)}), bf16[8,2,4,8,1024]{4,3,2,1,0:T(8,128)(2,1)S(1)}, u32[]{:S(2)}, u32[]{:S(2)}) async-start(bf16[8,2,4,8,1024]{4,3,2,1,0:T(8,128)(2,1)} %bitcast.127), calls=%async_computation.1 | async-start | bytes 2097152 | tf_op jit(solution)/shard_map/all_to_all | solution.py:12
  68.9 6.6 %collective-permute-start.11 = (bf16[4,8,8,1024]{3,2,0,1:T(8,128)(2,1)S(1)}, bf16[4,8,8,1024]{3,2,0,1:T(8,128)(2,1)S(1)}, u32[]{:S(2)}, u32[]{:S(2)}) collective-permute-start(bf16[4,8,8,1024]{3,2,0,1:T(8,128)(2,1)S(1)} %fusion.6), channel_id=1, source_target_pairs={{0,1},{1,0},{2,3},{3,2},{4,5},{5,4},{6,7},{7,6},{8,9},{9,8},{10,11... | collective-permute-start | bytes 1572872 | tf_op jit(solution)/shard_map/ppermute | solution.py:17
  70.5 10.0 %collective-permute-start.18 = (bf16[128,1024]{1,0:T(8,128)(2,1)S(1)}, bf16[128,1024]{1,0:T(8,128)(2,1)S(1)}, u32[]{:S(2)}, u32[]{:S(2)}) collective-permute-start(bf16[128,1024]{1,0:T(8,128)(2,1)S(1)} %get-tuple-element.51), channel_id=1, source_target_pairs={{0,192},{64,0},{128,64},{192,128},{1,193},{65,1},{129,65},{193,129... | collective-permute-start | bytes 786440 | tf_op jit(solution)/shard_map/ppermute | solution.py:17
  74.3 9.6 %collective-permute-start.20 = (bf16[128,1024]{1,0:T(8,128)(2,1)S(1)}, bf16[128,1024]{1,0:T(8,128)(2,1)S(1)}, u32[]{:S(2)}, u32[]{:S(2)}) collective-permute-start(bf16[128,1024]{1,0:T(8,128)(2,1)S(1)} %get-tuple-element.52), channel_id=1, source_target_pairs={{0,64},{64,128},{128,192},{192,0},{1,65},{65,129},{129,193},{193,1... | collective-permute-start | bytes 786440 | tf_op jit(solution)/shard_map/ppermute | solution.py:17
  75.8 11.1 %collective-permute-start.12 = (bf16[8,8,1024]{2,1,0:T(8,128)(2,1)S(1)}, bf16[8,8,1024]{2,1,0:T(8,128)(2,1)S(1)}, u32[]{:S(2)}, u32[]{:S(2)}) collective-permute-start(bf16[8,8,1024]{2,1,0:T(8,128)(2,1)S(1)} %get-tuple-element.53), channel_id=1, source_target_pairs={{0,6},{2,0},{4,2},{6,4},{1,7},{3,1},{5,3},{7,5},{8,14},{10,8},{12,... | collective-permute-start | bytes 393224 | tf_op jit(solution)/shard_map/ppermute | solution.py:17
  76.4 10.5 %collective-permute-start.14 = (bf16[8,8,1024]{2,1,0:T(8,128)(2,1)S(1)}, bf16[8,8,1024]{2,1,0:T(8,128)(2,1)S(1)}, u32[]{:S(2)}, u32[]{:S(2)}) collective-permute-start(bf16[8,8,1024]{2,1,0:T(8,128)(2,1)S(1)} %get-tuple-element.54), channel_id=1, source_target_pairs={{0,2},{2,4},{4,6},{6,0},{1,3},{3,5},{5,7},{7,1},{8,10},{10,12},{12... | collective-permute-start | bytes 393224 | tf_op jit(solution)/shard_map/ppermute | solution.py:17
  77.9 9.0 %collective-permute-start.13 = (bf16[8,8,1024]{2,1,0:T(8,128)(2,1)S(1)}, bf16[8,8,1024]{2,1,0:T(8,128)(2,1)S(1)}, u32[]{:S(2)}, u32[]{:S(2)}) collective-permute-start(bf16[8,8,1024]{2,1,0:T(8,128)(2,1)S(1)} %get-tuple-element.55), channel_id=1, source_target_pairs={{0,4},{2,6},{4,0},{6,2},{1,5},{3,7},{5,1},{7,3},{8,12},{10,14},{12... | collective-permute-start | bytes 393224 | tf_op jit(solution)/shard_map/ppermute | solution.py:17
  84.9 26.0 %collective-permute-start.19 = (bf16[2,128,1024]{2,1,0:T(8,128)(2,1)}, bf16[2,128,1024]{2,1,0:T(8,128)(2,1)S(1)}, u32[]{:S(2)}, u32[]{:S(2)}) collective-permute-start(bf16[2,128,1024]{2,1,0:T(8,128)(2,1)} %get-tuple-element.47), channel_id=1, source_target_pairs={{0,192},{64,0},{128,64},{192,128},{1,193},{65,1},{129,65},{193,129... | collective-permute-start | bytes 1572872 | tf_op jit(solution)/shard_map/ppermute | solution.py:17
  85.2 25.7 %collective-permute-start.21 = (bf16[2,128,1024]{2,1,0:T(8,128)(2,1)}, bf16[2,128,1024]{2,1,0:T(8,128)(2,1)S(1)}, u32[]{:S(2)}, u32[]{:S(2)}) collective-permute-start(bf16[2,128,1024]{2,1,0:T(8,128)(2,1)} %get-tuple-element.48), channel_id=1, source_target_pairs={{0,64},{64,128},{128,192},{192,0},{1,65},{65,129},{129,193},{193,1... | collective-permute-start | bytes 1572872 | tf_op jit(solution)/shard_map/ppermute | solution.py:17
  87.7 16.5 %collective-permute-start.17 = (f32[64,256]{1,0:T(8,128)}, f32[64,256]{1,0:T(8,128)}, u32[]{:S(2)}, u32[]{:S(2)}) collective-permute-start(f32[64,256]{1,0:T(8,128)} %get-tuple-element.58), channel_id=1, source_target_pairs={{0,64},{64,128},{128,192},{192,0},{1,65},{65,129},{129,193},{193,1... | collective-permute-start | bytes 196616 | tf_op jit(solution)/shard_map/ppermute | solution.py:17
  87.7 15.0 %collective-permute-start.16 = (f32[64,256]{1,0:T(8,128)}, f32[64,256]{1,0:T(8,128)}, u32[]{:S(2)}, u32[]{:S(2)}) collective-permute-start(f32[64,256]{1,0:T(8,128)} %get-tuple-element.59), channel_id=1, source_target_pairs={{0,128},{64,192},{128,0},{192,64},{1,129},{65,193},{129,1},{193,65... | collective-permute-start | bytes 196616 | tf_op jit(solution)/shard_map/ppermute | solution.py:17
  90.7 10.6 %collective-permute-start.15 = (f32[64,256]{1,0:T(8,128)}, f32[64,256]{1,0:T(8,128)}, u32[]{:S(2)}, u32[]{:S(2)}) collective-permute-start(f32[64,256]{1,0:T(8,128)} %get-tuple-element.60), channel_id=1, source_target_pairs={{0,192},{64,0},{128,64},{192,128},{1,193},{65,1},{129,65},{193,129... | collective-permute-start | bytes 196616 | tf_op jit(solution)/shard_map/ppermute | solution.py:17
  92.5 18.4 %all-to-all-start.2 = ((bf16[8,8,1024]{2,1,0:T(8,128)(2,1)}), bf16[8,8,1024]{2,1,0:T(8,128)(2,1)S(1)}, u32[]{:S(2)}, u32[]{:S(2)}) async-start(bf16[8,8,1024]{2,1,0:T(8,128)(2,1)} %bitcast.22), calls=%async_computation.2 | async-start | bytes 262144 | tf_op jit(solution)/shard_map/all_to_all | solution.py:12
  (4 other events, 14.2 us)
